TPU v7x, 512 devices: a whole 4x8x8 slice. The times are simulated.
512 devices in a mesh: blk: 8 (over y_lo, core), team: 64 (over y_hi, x, z).
Axes of the slice: x: 4, y: 8 (y_hi: 2, y_lo: 4; y = y_hi * 4 + y_lo), z: 8, core: 2. Of those that a mesh axis runs over, the one named last changes fastest.
Arguments:
- features: bfloat16 [65536, 256], P(('blk', 'team')), may hold values from -6 to 6
- weight: bfloat16 [256, 256], replicated, may hold values from -0.375 to 0.375
- bias: float32 [256], replicated, may hold values from -3 to 3
- cotangent: bfloat16 [65536, 256], P(('blk', 'team')), may hold values from -6 to 6
- adj_cols: int32 [64, 8, 8, 12], P('team', None, 'blk'), may hold values from 0 to 63, as said below
- adj_vals: bfloat16 [64, 8, 8, 12, 128, 128], P('team', None, 'blk'), as said below
Outputs:
- hidden: bfloat16 [65536, 256], P(('blk', 'team'))
- grad_input: bfloat16 [65536, 256], P(('blk', 'team'))
- grad_weight: float32 [256, 256], replicated
- grad_bias: float32 [256], replicated
Inputs may be any that keep to these rules, and one draw needn't show every extreme that they name: `adj_cols`: for every node panel and column group the 12 entries are distinct. Block (i, j) of A is listed exactly when block (j, i) is, every column panel is listed by exactly 12 row panels of each column group, and A is symmetric. `adj_vals`: the block listed for panels (i, j) is the transpose of the block listed for (j, i), so A is symmetric.
All inputs are finite; a program needn't handle non-finite values.
Results may differ from a plain program's by a relative error of at most 0.0075.
Values may be sent and summed in bfloat16 or wider, within the bound.
No kernel may reach another device: no remote copies, remote signals or barrier semaphores. Data moves between devices by JAX's collectives and lax.ppermute only.
A program may use at most 64 MiB of HBM per device.

v0:
```python
import jax
import jax.numpy as jnp
from jax import lax
from jax.sharding import Mesh
from jax.sharding import PartitionSpec as P

BLK_AXES = ("y_lo", "core")
TEAM_AXES = ("y_hi", "x", "z")
PLANE = ("x", "z")
ALL_AXES = BLK_AXES + TEAM_AXES


def fine_mesh(mesh):
    blk = mesh.shape["blk"]
    team = mesh.shape["team"]
    sizes = (blk // 2, 2, 2, 4, team // 8)
    return Mesh(mesh.devices.reshape(sizes), ALL_AXES)


def gather_team(rows):
    other = lax.ppermute(rows, "y_hi", perm=[(0, 1), (1, 0)])
    pair = jnp.stack([rows, other], axis=0)
    full = lax.all_gather(pair, PLANE, axis=0, tiled=True)
    return full.reshape(-1, rows.shape[1])


def member_slots(members, plane_size):
    my_hi = lax.axis_index("y_hi")
    return members % plane_size * 2 + (members // plane_size != my_hi).astype(jnp.int32)


def collect(panels, slots, adj_vals):
    block = adj_vals.shape[-1]
    width = panels.shape[1]
    stacked = panels.reshape(panels.shape[0] // block, block, width)
    picked = jnp.take(stacked, slots, axis=0)
    summed = jnp.einsum(
        "rkij,rkjf->rif", adj_vals[0, :, 0], picked, preferred_element_type=jnp.float32
    )
    return summed.reshape(-1, width)


def activation(value):
    return jax.nn.gelu(value, approximate=True)


def local(features, weight, bias, cotangent, adj_cols, adj_vals):
    plane_size = lax.psum(1, PLANE)
    slots = member_slots(adj_cols[0, :, 0, :], plane_size)
    product = jnp.dot(features, weight, preferred_element_type=jnp.float32).astype(jnp.bfloat16)
    gathered = gather_team(product)
    partial_rows = collect(gathered, slots, adj_vals)
    summed = lax.psum_scatter(partial_rows, BLK_AXES, scatter_dimension=0, tiled=True)
    pre = summed + bias[None, :]
    activated, pullback = jax.vjp(activation, pre)
    hidden = activated.astype(jnp.bfloat16)
    pulled = pullback(cotangent.astype(jnp.float32))[0].astype(jnp.bfloat16)
    pulled_group = gather_team(pulled)
    partial_back = collect(pulled_group, slots, adj_vals)
    spread = lax.psum_scatter(partial_back, BLK_AXES, scatter_dimension=0, tiled=True).astype(
        jnp.bfloat16
    )
    grad_input = jnp.dot(spread, weight.T, preferred_element_type=jnp.float32).astype(jnp.bfloat16)
    local_weight = lax.dot_general(
        features, spread, (((0,), (0,)), ((), ())), preferred_element_type=jnp.float32
    )
    local_bias = jnp.sum(pulled.astype(jnp.float32), axis=0)
    both = jnp.concatenate([local_weight, local_bias[None, :]], axis=0)
    both = lax.psum(both, PLANE)
    both = lax.psum(both, ("y_lo", "y_hi", "core"))
    grad_weight = both[:-1]
    grad_bias = both[-1]
    return (hidden, grad_input, grad_weight, grad_bias)


def solution(mesh):
    fine = fine_mesh(mesh)
    rows = P(ALL_AXES, None)
    return jax.shard_map(
        local,
        mesh=fine,
        in_specs=(
            rows,
            P(),
            P(),
            rows,
            P(TEAM_AXES, None, BLK_AXES, None),
            P(TEAM_AXES, None, BLK_AXES, None, None, None),
        ),
        out_specs=(rows, rows, P(), P()),
        check_vma=False,
    )
```

profile of v0, /device:TPU:1, one launch (start us, length us, event | category | flops | bytes accessed | tf_op | source)
XLA Modules:
  0.0 590.6 jit_solution(9726838023997011577)
XLA Ops:
  7.2 1.2 convolution_convert_fusion.1
  8.5 8.3 %collective-permute-start = (bf16[128,256]{1,0:T(8,128)(2,1)S(1)}, bf16[128,256]{1,0:T(8,128)(2,1)S(1)}, u32[]{:S(2)}, u32[]{:S(2)}) collective-permute-start(bf16[128,256]{1,0:T(8,128)(2,1)S(1)} %convolution_convert_fusion.1), channel_id=1, source_target_pairs={{0,32},{32,0},{1,33},{33,1},{2,34},{34,2},{3,35},{35,3},{4,36},{36... | collective-permute-start | bytes 196616 | tf_op jit(solution)/shard_map/ppermute | solution.py:21
  16.8 1.7 collective-permute-done
  18.5 0.7 pad_maximum_fusion.1
  19.2 0.7 compare_and_fusion
  20.0 91.1 %all-gather.3.cloned.1.call-done = bf16[64,128,256]{2,1,0:T(8,128)(2,1)} async-done(((bf16[2,128,256]{2,1,0:T(8,128)(2,1)}), bf16[64,128,256]{2,1,0:T(8,128)(2,1)}) %all-gather.3.cloned.1.call-update) | async-done | bytes 4194320 | tf_op jit(solution)/shard_map/all_gather | solution.py:23
  111.1 8.2 %gather_fusion = bf16[96,128,256]{2,1,0:T(8,128)(2,1)} fusion(bf16[64,128,256]{2,1,0:T(8,128)(2,1)} %all-gather.3.cloned.1.call-done, s32[1024]{0:T(1024)S(1)} %pad_clamp_fusion), kind=kCustom, calls=%fused_computation.clone | custom fusion | bytes 12583296 | tf_op jit(solution)/shard_map/jit(_take)/gather | solution.py:36
  119.3 5.2 fusion.2
  124.6 38.0 %reduce-scatter.3.cloned.1.call-done = f32[128,256]{1,0:T(8,128)} async-done(((f32[1024,256]{1,0:T(8,128)}), f32[128,256]{1,0:T(8,128)}) %reduce-scatter.3.cloned.1.call-update) | async-done | bytes 131088 | tf_op jit(solution)/shard_map/reduce_scatter | solution.py:53
  162.5 1.6 convert_reduce_fusion
  164.2 5.5 collective-permute-start.1
  169.6 3.7 collective-permute-done.1
  173.3 0.7 pad_maximum_fusion.2
  174.1 86.9 %all-gather.5.cloned.1.call-done = bf16[64,128,256]{2,1,0:T(8,128)(2,1)} async-done(((bf16[2,128,256]{2,1,0:T(8,128)(2,1)}), bf16[64,128,256]{2,1,0:T(8,128)(2,1)}) %all-gather.5.cloned.1.call-update) | async-done | bytes 4194320 | tf_op jit(solution)/shard_map/all_gather | solution.py:23
  260.9 8.2 %gather_fusion.1 = bf16[96,128,256]{2,1,0:T(8,128)(2,1)} fusion(bf16[64,128,256]{2,1,0:T(8,128)(2,1)} %all-gather.5.cloned.1.call-done, s32[1024]{0:T(1024)S(1)} %pad_clamp_fusion), kind=kCustom, calls=%fused_computation.1.clone | custom fusion | bytes 12583296 | tf_op jit(solution)/shard_map/jit(_take)/gather | solution.py:36
  269.1 5.2 fusion
  274.4 38.0 %reduce-scatter.5.cloned.1.call-done = f32[128,256]{1,0:T(8,128)} async-done(((f32[1024,256]{1,0:T(8,128)}), f32[128,256]{1,0:T(8,128)}) %reduce-scatter.5.cloned.1.call-update) | async-done | bytes 131088 | tf_op jit(solution)/shard_map/reduce_scatter | solution.py:60
  312.3 1.1 convolution_bitcast_fusion
  313.5 0.7 pad_maximum_fusion
  314.3 153.2 %all-reduce.3.cloned.1.call-done = f32[257,256]{1,0:T(8,128)} async-done(((f32[257,256]{1,0:T(8,128)}), f32[257,256]{1,0:T(8,128)}) %all-reduce.3.cloned.1.call-update) | async-done | bytes 263184 | tf_op jit(solution)/shard_map/psum | solution.py:69
  467.5 1.7 convolution_convert_fusion
  469.2 111.6 %all-reduce.5.cloned.1.call-done = f32[257,256]{1,0:T(8,128)} async-done(((f32[257,256]{1,0:T(8,128)}), f32[257,256]{1,0:T(8,128)}) %all-reduce.5.cloned.1.call-update) | async-done | bytes 263184 | tf_op jit(solution)/shard_map/psum | solution.py:70
  580.8 1.3 slice.13
  582.1 1.7 slice.12
  (24 shorter events, 0.5 us)
Async XLA Ops:
  7.2 112.1 %copy-start = (bf16[1,8,1,12,128,128]{5,4,3,2,1,0:T(8,128)(2,1)S(1)}, bf16[1,8,1,12,128,128]{5,4,3,2,1,0:T(8,128)(2,1)}, u32[]{:S(2)}) copy-start(bf16[1,8,1,12,128,128]{5,4,3,2,1,0:T(8,128)(2,1)} %param.13) | copy-start | bytes 9437188
  7.2 103.9 %all-gather.3.cloned.1.call-start = ((), (), s32[]{:S(2)}) async-start(), calls=%async_computation.2 | async-start | bytes 4325376 | tf_op jit(solution)/shard_map/all_gather | solution.py:23
  8.5 10.0 %collective-permute-start = (bf16[128,256]{1,0:T(8,128)(2,1)S(1)}, bf16[128,256]{1,0:T(8,128)(2,1)S(1)}, u32[]{:S(2)}, u32[]{:S(2)}) collective-permute-start(bf16[128,256]{1,0:T(8,128)(2,1)S(1)} %convolution_convert_fusion.1), channel_id=1, source_target_pairs={{0,32},{32,0},{1,33},{33,1},{2,34},{34,2},{3,35},{35,3},{4,36},{36... | collective-permute-start | bytes 196616 | tf_op jit(solution)/shard_map/ppermute | solution.py:21
  19.2 143.4 %reduce-scatter.3.cloned.1.call-start = ((), (), s32[]{:S(2)}) async-start(), calls=%async_computation.3 | async-start | bytes 1179648 | tf_op jit(solution)/shard_map/reduce_scatter | solution.py:53
  119.3 43.2 %copy-start.3 = (bf16[128,256]{1,0:T(8,128)(2,1)S(1)}, bf16[128,256]{1,0:T(8,128)(2,1)}, u32[]{:S(2)}) copy-start(bf16[128,256]{1,0:T(8,128)(2,1)} %param.11) | copy-start | bytes 196612
  119.3 43.2 %copy-start.4 = (f32[256]{0:T(256)S(1)}, f32[256]{0:T(256)}, u32[]{:S(2)}) copy-start(f32[256]{0:T(256)} %param.10) | copy-start | bytes 3076
  124.5 136.4 %all-gather.5.cloned.1.call-start = ((), (), s32[]{:S(2)}) async-start(), calls=%async_computation.4 | async-start | bytes 4325376 | tf_op jit(solution)/shard_map/all_gather | solution.py:23
  164.2 9.1 %collective-permute-start.1 = (bf16[128,256]{1,0:T(8,128)(2,1)S(1)}, bf16[128,256]{1,0:T(8,128)(2,1)S(1)}, u32[]{:S(2)}, u32[]{:S(2)}) collective-permute-start(bf16[128,256]{1,0:T(8,128)(2,1)S(1)} %get-tuple-element.6), channel_id=1, source_target_pairs={{0,32},{32,0},{1,33},{33,1},{2,34},{34,2},{3,35},{35,3},{4,36},{36... | collective-permute-start | bytes 196616 | tf_op jit(solution)/shard_map/ppermute | solution.py:21
  174.0 138.3 %reduce-scatter.5.cloned.1.call-start = ((), (), s32[]{:S(2)}) async-start(), calls=%async_computation.5 | async-start | bytes 1179648 | tf_op jit(solution)/shard_map/reduce_scatter | solution.py:60
  269.1 43.2 %copy-start.2 = (bf16[128,256]{1,0:T(8,128)(2,1)S(1)}, bf16[128,256]{1,0:T(8,128)(2,1)}, u32[]{:S(2)}) copy-start(bf16[128,256]{1,0:T(8,128)(2,1)} %param.8) | copy-start | bytes 196612
  269.1 198.3 %copy-start.1 = (bf16[256,256]{1,0:T(8,128)(2,1)S(1)}, bf16[256,256]{1,0:T(8,128)(2,1)}, u32[]{:S(2)}) copy-start(bf16[256,256]{1,0:T(8,128)(2,1)} %param.9) | copy-start | bytes 393220
  274.3 193.1 %all-reduce.3.cloned.1.call-start = ((), (), s32[]{:S(2)}) async-start(), calls=%async_computation.6 | async-start | bytes 540672 | tf_op jit(solution)/shard_map/psum | solution.py:69
  314.2 266.6 %all-reduce.5.cloned.1.call-start = ((), (), s32[]{:S(2)}) async-start(), calls=%async_computation.7 | async-start | bytes 540672 | tf_op jit(solution)/shard_map/psum | solution.py:70
Sparse Core Ops, SparseCore 0:
  19.3 91.7 all-gather.2
  124.6 37.8 reduce-scatter.2
  174.1 86.7 all-gather.4
  274.5 37.8 reduce-scatter.4
  315.6 151.7 all-reduce.2
  469.6 111.1 all-reduce.4
where the time goes:
time: 591 us
  waiting for transfers between devices  524 us (89%)
  local copies, waits for them, and re-layouts  19.4 us (3%)
  matrix products  14.5 us (2%)
  between operations  14.2 us (2%)
  starting transfers between devices  14 us (2%)
    all_gather x2, waiting for transfers between devices, gather_team(): full = lax.all_gather(pair, PLANE, axis=0, tiled=True)  178 us
    psum x1, waiting for transfers between devices, local(): both = lax.psum(both, PLANE)  153 us
    psum x1, waiting for transfers between devices, local(): both = lax.psum(both, ('y_lo', 'y_hi', 'core'))  112 us
    reduce_scatter x1, waiting for transfers between devices, local(): lax.psum_scatter(partial_back, BLK_AXES, scatter_dimension=0, tiled=True)  38 us
    reduce_scatter x1, waiting for transfers between devices, local(): lax.psum_scatter(partial_rows, BLK_AXES, scatter_dimension=0, tiled=True)  38 us
    gather x2, local copies, waits for them, and re-layouts, collect(): picked = jnp.take(stacked, slots, axis=0)  16.4 us
    ppermute x2, starting transfers between devices, gather_team(): other = lax.ppermute(rows, 'y_hi', perm=[(0, 1), (1, 0)])  13.7 us
  transfers between devices with their start and end apart: 8, of which 8 were waited for; matrix products, arithmetic and copies ran while one was open for 0% of the time, Pallas kernels for 0%

commit v1 on v0

--- a/solution.py
+++ b/solution.py
@@ -20,7 +20,10 @@
 def gather_team(rows):
     other = lax.ppermute(rows, "y_hi", perm=[(0, 1), (1, 0)])
     pair = jnp.stack([rows, other], axis=0)
-    full = lax.all_gather(pair, PLANE, axis=0, tiled=True)
+    size = lax.axis_size(PLANE)
+    tiles = jnp.stack([pair for _ in range(size)])
+    tiles = lax.all_to_all(tiles, PLANE, split_axis=0, concat_axis=0)
+    full = jnp.concatenate(tiles, axis=0)
     return full.reshape(-1, rows.shape[1])
 
 

time: 591 us -> 622 us (1.052)
  blocking collectives: 0 us -> 95 us
  waiting for transfers between devices: 524 us -> 446 us
  starting transfers between devices: 14 us -> 26.9 us
    all_gather x2 -> x0, waiting for transfers between devices: 178 us -> none  [gather_team(): full = lax.all_gather(pair, PLANE, axis=0, tiled=True)]
    all_to_all x0 -> x1, blocking collectives: none -> 95 us  [gather_team(): tiles = lax.all_to_all(tiles, PLANE, split_axis=0, concat_axis=0)]
    all_to_all x0 -> x1, waiting for transfers between devices: none -> 94.7 us  [gather_team(): tiles = lax.all_to_all(tiles, PLANE, split_axis=0, concat_axis=0)]
    all_to_all x0 -> x1, starting transfers between devices: none -> 13 us  [gather_team(): tiles = lax.all_to_all(tiles, PLANE, split_axis=0, concat_axis=0)]
  transfers between devices with their start and end apart: 8 -> 7, of which waited for: 8 -> 7; matrix products, arithmetic and copies ran while one was open for 0% -> 0% of each run, Pallas kernels for 0% -> 0%
where the time goes in v1:
time: 622 us; the launch traced here: 621 us
  waiting for transfers between devices  446 us (72%)
  blocking collectives  95 us (15%)
  starting transfers between devices  26.9 us (4%)
  local copies, waits for them, and re-layouts  22.4 us (4%)
  matrix products  14.5 us (2%)
  between operations  13.9 us (2%)
    psum x1, waiting for transfers between devices, local(): both = lax.psum(both, PLANE)  153 us
    psum x1, waiting for transfers between devices, local(): both = lax.psum(both, ('y_lo', 'y_hi', 'core'))  112 us
    all_to_all x1, blocking collectives, gather_team(): tiles = lax.all_to_all(tiles, PLANE, split_axis=0, concat_axis=0)  95 us
    all_to_all x1, waiting for transfers between devices, gather_team(): tiles = lax.all_to_all(tiles, PLANE, split_axis=0, concat_axis=0)  94.7 us
    reduce_scatter x1, waiting for transfers between devices, local(): lax.psum_scatter(partial_back, BLK_AXES, scatter_dimension=0, tiled=True)  44 us
    reduce_scatter x1, waiting for transfers between devices, local(): lax.psum_scatter(partial_rows, BLK_AXES, scatter_dimension=0, tiled=True)  37 us
    gather x2, local copies, waits for them, and re-layouts, collect(): picked = jnp.take(stacked, slots, axis=0)  16.4 us
    ppermute x2, starting transfers between devices, gather_team(): other = lax.ppermute(rows, 'y_hi', perm=[(0, 1), (1, 0)])  13.8 us
  transfers between devices with their start and end apart: 7, of which 7 were waited for; matrix products, arithmetic and copies ran while one was open for 0% of the time, Pallas kernels for 0%

profile of v1, /device:TPU:1, one launch (start us, length us, event | category | flops | bytes accessed | tf_op | source)
XLA Modules:
  0.0 621.3 jit_solution(13930558632110600693)
XLA Ops:
  7.2 1.2 convolution_convert_fusion.1
  8.4 8.3 %collective-permute-start = (bf16[128,256]{1,0:T(8,128)(2,1)S(1)}, bf16[128,256]{1,0:T(8,128)(2,1)S(1)}, u32[]{:S(2)}, u32[]{:S(2)}) collective-permute-start(bf16[128,256]{1,0:T(8,128)(2,1)S(1)} %convolution_convert_fusion.1), channel_id=1, source_target_pairs={{0,32},{32,0},{1,33},{33,1},{2,34},{34,2},{3,35},{35,3},{4,36},{36... | collective-permute-start | bytes 196616 | tf_op jit(solution)/shard_map/ppermute | solution.py:21
  16.7 1.7 collective-permute-done
  18.5 2.5 stack.19
  20.9 13.0 %all-to-all-start = ((bf16[32,2,128,256]{3,2,1,0:T(8,128)(2,1)}), bf16[32,2,128,256]{3,2,1,0:T(8,128)(2,1)}, u32[]{:S(2)}, u32[]{:S(2)}) async-start(bf16[32,2,128,256]{3,2,1,0:T(8,128)(2,1)} %stack.19), calls=%async_computation | async-start | bytes 8388608 | tf_op jit(solution)/shard_map/all_to_all | solution.py:25
  34.1 94.7 %all-to-all-done = bf16[32,2,128,256]{3,2,1,0:T(8,128)(2,1)} async-done(((bf16[32,2,128,256]{3,2,1,0:T(8,128)(2,1)}), bf16[32,2,128,256]{3,2,1,0:T(8,128)(2,1)}, u32[]{:S(2)}, u32[]{:S(2)}) %all-to-all-start) | async-done | bytes 4194336 | tf_op jit(solution)/shard_map/all_to_all | solution.py:25
  128.8 8.2 %gather_fusion = bf16[96,128,256]{2,1,0:T(8,128)(2,1)} fusion(bf16[64,128,256]{2,1,0:T(8,128)(2,1)} %bitcast.3, s32[1024]{0:T(1024)S(1)} %pad_clamp_fusion), kind=kCustom, calls=%fused_computation.clone | custom fusion | bytes 12583296 | tf_op jit(solution)/shard_map/jit(_take)/gather | solution.py:39
  137.0 5.2 fusion.2
  142.3 37.0 %reduce-scatter.3.cloned.1.call-done = f32[128,256]{1,0:T(8,128)} async-done(((f32[1024,256]{1,0:T(8,128)}), f32[128,256]{1,0:T(8,128)}) %reduce-scatter.3.cloned.1.call-update) | async-done | bytes 131088 | tf_op jit(solution)/shard_map/reduce_scatter | solution.py:56
  179.3 1.6 convert_reduce_fusion
  180.9 5.5 collective-permute-start.1
  186.4 3.8 collective-permute-done.1
  190.3 0.5 stack.23
  190.8 95.0 %all_to_all.10 = bf16[32,2,128,256]{3,2,1,0:T(8,128)(2,1)} all-to-all(bf16[32,2,128,256]{3,2,1,0:T(8,128)(2,1)S(1)} %stack.23), channel_id=1, replica_groups=mesh['y_lo'=4,'core'=2,'y_hi'=2,'x'=4,'z'=8] {'x','z'}, dimensions={0} | all-to-all | bytes 8388608 | tf_op jit(solution)/shard_map/all_to_all | solution.py:25
  285.7 8.2 %gather_fusion.1 = bf16[96,128,256]{2,1,0:T(8,128)(2,1)} fusion(bf16[64,128,256]{2,1,0:T(8,128)(2,1)} %bitcast.34, s32[1024]{0:T(1024)S(1)} %pad_clamp_fusion), kind=kCustom, calls=%fused_computation.1.clone | custom fusion | bytes 12583296 | tf_op jit(solution)/shard_map/jit(_take)/gather | solution.py:39
  293.9 5.2 fusion
  299.2 44.0 %reduce-scatter.5.cloned.1.call-done = f32[128,256]{1,0:T(8,128)} async-done(((f32[1024,256]{1,0:T(8,128)}), f32[128,256]{1,0:T(8,128)}) %reduce-scatter.5.cloned.1.call-update) | async-done | bytes 131088 | tf_op jit(solution)/shard_map/reduce_scatter | solution.py:63
  343.2 1.1 convolution_bitcast_fusion
  344.3 0.7 pad_maximum_fusion
  345.1 153.4 %all-reduce.3.cloned.1.call-done = f32[257,256]{1,0:T(8,128)} async-done(((f32[257,256]{1,0:T(8,128)}), f32[257,256]{1,0:T(8,128)}) %all-reduce.3.cloned.1.call-update) | async-done | bytes 263184 | tf_op jit(solution)/shard_map/psum | solution.py:72
  498.5 1.7 convolution_convert_fusion
  500.2 111.6 %all-reduce.5.cloned.1.call-done = f32[257,256]{1,0:T(8,128)} async-done(((f32[257,256]{1,0:T(8,128)}), f32[257,256]{1,0:T(8,128)}) %all-reduce.5.cloned.1.call-update) | async-done | bytes 263184 | tf_op jit(solution)/shard_map/psum | solution.py:73
  611.9 1.3 slice.13
  613.1 1.7 slice.12
  (25 shorter events, 0.4 us)
Async XLA Ops:
  7.2 129.8 %copy-start = (bf16[1,8,1,12,128,128]{5,4,3,2,1,0:T(8,128)(2,1)S(1)}, bf16[1,8,1,12,128,128]{5,4,3,2,1,0:T(8,128)(2,1)}, u32[]{:S(2)}) copy-start(bf16[1,8,1,12,128,128]{5,4,3,2,1,0:T(8,128)(2,1)} %param.13) | copy-start | bytes 9437188
  8.4 10.0 %collective-permute-start = (bf16[128,256]{1,0:T(8,128)(2,1)S(1)}, bf16[128,256]{1,0:T(8,128)(2,1)S(1)}, u32[]{:S(2)}, u32[]{:S(2)}) collective-permute-start(bf16[128,256]{1,0:T(8,128)(2,1)S(1)} %convolution_convert_fusion.1), channel_id=1, source_target_pairs={{0,32},{32,0},{1,33},{33,1},{2,34},{34,2},{3,35},{35,3},{4,36},{36... | collective-permute-start | bytes 196616 | tf_op jit(solution)/shard_map/ppermute | solution.py:21
  18.5 15.5 %copy-start.4 = (s32[1,8,1,12]{3,2,1,0:T(1,128)S(1)}, s32[1,8,1,12]{3,2,1,0:T(1,128)}, u32[]{:S(2)}) copy-start(s32[1,8,1,12]{3,2,1,0:T(1,128)} %param.12) | copy-start | bytes 1156
  20.9 107.9 %all-to-all-start = ((bf16[32,2,128,256]{3,2,1,0:T(8,128)(2,1)}), bf16[32,2,128,256]{3,2,1,0:T(8,128)(2,1)}, u32[]{:S(2)}, u32[]{:S(2)}) async-start(bf16[32,2,128,256]{3,2,1,0:T(8,128)(2,1)} %stack.19), calls=%async_computation | async-start | bytes 8388608 | tf_op jit(solution)/shard_map/all_to_all | solution.py:25
  33.9 145.3 %reduce-scatter.3.cloned.1.call-start = ((), (), s32[]{:S(2)}) async-start(), calls=%async_computation.4 | async-start | bytes 1179648 | tf_op jit(solution)/shard_map/reduce_scatter | solution.py:56
  137.0 42.3 %copy-start.3 = (bf16[128,256]{1,0:T(8,128)(2,1)S(1)}, bf16[128,256]{1,0:T(8,128)(2,1)}, u32[]{:S(2)}) copy-start(bf16[128,256]{1,0:T(8,128)(2,1)} %param.11) | copy-start | bytes 196612
  137.0 42.3 %copy-start.5 = (f32[256]{0:T(256)S(1)}, f32[256]{0:T(256)}, u32[]{:S(2)}) copy-start(f32[256]{0:T(256)} %param.10) | copy-start | bytes 3076
  142.2 200.9 %reduce-scatter.5.cloned.1.call-start = ((), (), s32[]{:S(2)}) async-start(), calls=%async_computation.5 | async-start | bytes 1179648 | tf_op jit(solution)/shard_map/reduce_scatter | solution.py:63
  180.9 9.3 %collective-permute-start.1 = (bf16[128,256]{1,0:T(8,128)(2,1)S(1)}, bf16[128,256]{1,0:T(8,128)(2,1)S(1)}, u32[]{:S(2)}, u32[]{:S(2)}) collective-permute-start(bf16[128,256]{1,0:T(8,128)(2,1)S(1)} %get-tuple-element.6), channel_id=1, source_target_pairs={{0,32},{32,0},{1,33},{33,1},{2,34},{34,2},{3,35},{35,3},{4,36},{36... | collective-permute-start | bytes 196616 | tf_op jit(solution)/shard_map/ppermute | solution.py:21
  293.9 49.2 %copy-start.2 = (bf16[128,256]{1,0:T(8,128)(2,1)S(1)}, bf16[128,256]{1,0:T(8,128)(2,1)}, u32[]{:S(2)}) copy-start(bf16[128,256]{1,0:T(8,128)(2,1)} %param.8) | copy-start | bytes 196612
  293.9 204.5 %copy-start.1 = (bf16[256,256]{1,0:T(8,128)(2,1)S(1)}, bf16[256,256]{1,0:T(8,128)(2,1)}, u32[]{:S(2)}) copy-start(bf16[256,256]{1,0:T(8,128)(2,1)} %param.9) | copy-start | bytes 393220
  299.2 199.3 %all-reduce.3.cloned.1.call-start = ((), (), s32[]{:S(2)}) async-start(), calls=%async_computation.6 | async-start | bytes 540672 | tf_op jit(solution)/shard_map/psum | solution.py:72
  345.0 266.8 %all-reduce.5.cloned.1.call-start = ((), (), s32[]{:S(2)}) async-start(), calls=%async_computation.7 | async-start | bytes 540672 | tf_op jit(solution)/shard_map/psum | solution.py:73
Sparse Core Ops, SparseCore 0:
  142.3 36.8 reduce-scatter.2
  299.3 43.8 reduce-scatter.4
  346.6 151.7 all-reduce.2
  500.6 111.1 all-reduce.4
